TPU v7x, 256 devices: a whole 4x4x8 slice. The times are simulated.
256 devices in a mesh: section: 2 (over core), srv: 32 (over x, z), tp: 4 (over y).
Axes of the slice: x: 4, y: 4, z: 8, core: 2. Of those that a mesh axis runs over, the one named last changes fastest.
Arguments:
- queries: bfloat16 [8192, 4096], P(('section', 'srv'), 'tp'), may hold values from -40 to 40
- keys: bfloat16 [8192, 512], P(('section', 'srv'), 'tp'), may hold values from -40 to 40
- values: bfloat16 [8192, 512], P(('section', 'srv'), 'tp'), may hold values from -6 to 6
- residual: bfloat16 [8192, 4096], P(('section', 'srv'), 'tp'), may hold values from -6 to 6
- out_weight: bfloat16 [4096, 4096], P('tp', ('section', 'srv')), may hold values from -0.1875 to 0.1875
- norm_gain: float32 [4096], P('tp'), may hold values from 0.25 to 1.75
- level_shift: float32 [8, 4096], P(None, 'tp'), may hold values from -3 to 3
- doc_lengths: int32 [2, 4], P('section'), may hold values from 1 to 128, 256 in all within a row
- noise_level: int32 [2, 4], P('section'), may hold values from 0 to 7
Outputs:
- normed: bfloat16 [8192, 4096], P(('section', 'srv'), 'tp')
Inputs may be any that keep to these rules, and one draw needn't show every extreme that they name: `doc_lengths`: each micro-batch's lengths sum to 256.
All inputs are finite; a program needn't handle non-finite values.
Results may differ from a plain program's by a relative error of at most 0.013.
Values may be sent and summed in bfloat16 or wider, within the bound.
A program may use at most 64 MiB of HBM per device.

v0:
```python
import jax
import jax.numpy as jnp
from jax import lax
from jax.sharding import PartitionSpec as P

D = 4096
HEAD_SIZE = 128
BLK = 16


def in_one_piece(arrays, axis, dim, along):
    ends, at = ([], 0)
    for a in arrays[:-1]:
        at += a.shape[along]
        ends.append(at)
    both = jnp.concatenate(arrays, axis=along)
    return tuple(jnp.split(lax.all_gather(both, axis, axis=dim, tiled=True), ends, axis=along))


def in_blocks(value, dim, length):
    dims = value.shape
    parts = value.reshape(*dims[:dim], length, dims[dim] // length, *dims[dim + 1 :])
    return jnp.moveaxis(parts, dim, 0)


def sent_and_summed(value, axis, dim):
    length = lax.axis_size(axis)
    parts = lax.all_to_all(in_blocks(value, dim, length), axis, 0, 0, tiled=True)
    return jnp.sum(parts.astype(jnp.float32), axis=0)


def from_everyone(value, axis):
    copies = jnp.broadcast_to(value, (lax.axis_size(axis), *value.shape))
    return lax.all_to_all(copies, axis, split_axis=0, concat_axis=0, tiled=True)


def of_everyone(value, axis):
    everything = from_everyone(value, axis)
    return jnp.sum(everything, axis=0)


def bounds(positions, starts, ends):
    member = (positions[:, None] >= starts[None, :]) & (positions[:, None] < ends[None, :])
    first = jnp.sum(jnp.where(member, starts[None, :], 0), axis=1)
    limit = (positions // BLK + 1) * BLK
    return (member, first, limit)


def make_absorb(query_block, first, limit, kv_heads, query_groups):
    rows = query_block.shape[0]
    scale = HEAD_SIZE ** (-0.5)
    grouped = (
        query_block.reshape(rows, kv_heads, query_groups, HEAD_SIZE)
        .transpose(1, 2, 0, 3)
        .reshape(kv_heads, query_groups * rows, HEAD_SIZE)
    )
    row_first = jnp.tile(first, query_groups)
    row_limit = jnp.tile(limit, query_groups)
    empty = (
        jnp.full((kv_heads, query_groups * rows), -1e30, jnp.float32),
        jnp.zeros((kv_heads, query_groups * rows), jnp.float32),
        jnp.zeros((kv_heads, query_groups * rows, HEAD_SIZE), jnp.float32),
    )

    def absorb(carry, pieces, start):
        key_piece, value_piece = pieces
        count = key_piece.shape[0]
        key_pos = jnp.arange(count, dtype=jnp.int32)
        mask = (key_pos[None, :] >= row_first[:, None]) & (key_pos[None, :] < row_limit[:, None])

        def update(state):
            best, total, summed = state
            key_heads = key_piece.reshape(count, kv_heads, HEAD_SIZE)
            value_heads = value_piece.reshape(count, kv_heads, HEAD_SIZE)
            scores = (
                jnp.einsum("kxd,jkd->kxj", grouped, key_heads, preferred_element_type=jnp.float32)
                * scale
            )
            scores = jnp.where(mask[None], scores, -1e30)
            new_best = jnp.maximum(best, jnp.max(scores, axis=-1))
            weights = jnp.where(mask[None], jnp.exp(scores - new_best[..., None]), 0.0)
            total = jnp.sum(weights, axis=-1)
            update_sum = jnp.einsum(
                "kxj,jkd->kxd",
                weights.astype(jnp.bfloat16),
                value_heads,
                preferred_element_type=jnp.float32,
            )
            return (new_best, total, update_sum)

        return lax.cond(jnp.any(mask), update, lambda state: state, carry)

    return (absorb, empty)


def finish(carry, rows, kv_heads, query_groups):
    best, total, summed = carry
    attended = (
        (summed / total[..., None])
        .reshape(kv_heads, query_groups, rows, HEAD_SIZE)
        .transpose(2, 0, 1, 3)
    )
    return attended.reshape(rows, kv_heads * query_groups * HEAD_SIZE).astype(jnp.bfloat16)


def on_device(
    queries, keys, values, residual, out_weight, norm_gain, level_shift, doc_lengths, noise_level
):
    rows = queries.shape[0]
    kv_heads = keys.shape[1] // HEAD_SIZE
    query_groups = queries.shape[1] // keys.shape[1]
    here = lax.axis_index("srv")
    lengths = doc_lengths[0] * BLK
    ends = jnp.cumsum(lengths)
    starts = ends - lengths
    positions = here * rows + jnp.arange(rows, dtype=jnp.int32)
    member, first, limit = bounds(positions, starts, ends)
    absorb, empty = make_absorb(queries, first, limit, kv_heads, query_groups)
    carry = absorb(empty, in_one_piece((keys, values), "srv", 0, 1), jnp.int32(0))
    attended = finish(carry, rows, kv_heads, query_groups)
    partial_sum = jnp.dot(
        attended,
        lax.all_gather(out_weight, ("section", "srv"), axis=1, tiled=True),
        preferred_element_type=jnp.float32,
    )
    share = sent_and_summed(partial_sum.astype(jnp.bfloat16), "tp", 1)
    hidden = residual.astype(jnp.float32) + share
    squares = of_everyone(jnp.sum(hidden * hidden, axis=1), "tp")
    inverse = lax.rsqrt(squares / D + 1e-06)
    level = jnp.sum(jnp.where(member, noise_level[0][None, :], 0), axis=1)
    onehot = (level[:, None] == jnp.arange(level_shift.shape[0], dtype=jnp.int32)[None, :]).astype(
        jnp.float32
    )
    shift = jnp.dot(onehot, level_shift)
    normed = hidden * inverse[:, None] * norm_gain[None, :] * (1.0 + shift)
    return normed.astype(jnp.bfloat16)


def solution(mesh):
    placed = (
        P(("section", "srv"), "tp"),
        P(("section", "srv"), "tp"),
        P(("section", "srv"), "tp"),
        P(("section", "srv"), "tp"),
        P("tp", ("section", "srv")),
        P("tp"),
        P(None, "tp"),
        P("section", None),
        P("section", None),
    )
    return jax.shard_map(
        on_device,
        mesh=mesh,
        in_specs=placed,
        out_specs=P(("section", "srv"), "tp"),
        check_vma=False,
    )
```

profile of v0, /device:TPU:1, one launch (start us, length us, event | category | flops | bytes accessed | tf_op | source)
XLA Modules:
  0.0 214.5 jit_solution(1870984475952749132)
XLA Ops:
  6.5 0.0 copy-start
  6.5 0.0 all-gather.3.cloned.1.call-start
  6.5 1.4 pad_maximum_fusion
  8.0 0.0 all-gather.3.cloned.1.call-update
  8.0 0.0 all-gather.5.cloned.1.call-start
  8.0 0.7 all-gather.5.cloned.1.call-update
  8.7 1.1 copy.23
  9.9 0.7 multiply_bitcast_fusion
  10.5 0.2 reduce-window.4
  10.7 0.7 fusion.18
  11.4 0.7 select_reduce_fusion
  12.1 8.8 %fusion.14 = (pred[1024,4096]{1,0:T(32,128)(4,1)}, pred[]{:T(512)}) fusion(s32[1024]{0:T(1024)S(1)} %broadcast_bitcast_fusion, s32[1024]{0:T(1024)S(1)} %broadcast_bitcast_fusion.1), kind=kLoop, calls=%fused_computation.16 | loop fusion | flops 16777215 | bytes 4202497 | tf_op jit(solution)/shard_map/and | solution.py:69
  21.6 66.1 %all-gather.3.cloned.1.call-done = bf16[4096,256]{1,0:T(8,128)(2,1)} async-done(((bf16[128,256]{1,0:T(8,128)(2,1)}), bf16[4096,256]{1,0:T(8,128)(2,1)}) %all-gather.3.cloned.1.call-update) | async-done | bytes 2097168 | tf_op jit(solution)/shard_map/all_gather | solution.py:17
  87.8 16.3 %conditional.1 = (f32[1,1024]{1,0:T(1,128)S(1)}, f32[1,1024,128]{2,1,0:T(8,128)S(1)}) conditional(s32[]{:T(128)} %convert_element_type.33, () %tuple.13, (bf16[1,8,128,128]{2,3,1,0:T(8,128)(2,1)S(1)}, bf16[4096,256]{1,0:T(8,128)(2,1)}, pred[1024,4096]{1,0:T(32,128)(4,1)}) %tuple.30), branch_computations={%region_3.4_spmd, %region_4.7_spmd} | conditional | flops 2202008576 | bytes 91512904 | solution.py:91
  87.8 0.0 copy-start.3
  87.8 0.2 copy.24
  88.0 0.0 copy-start.1
  88.0 6.0 %fusion = (f32[1024]{0:T(1024)S(1)}, f32[1024,4096]{1,0:T(8,128)S(1)}) fusion(pred[1024,4096]{1,0:T(32,128)(4,1)} %get-tuple-element.15, bf16[1024,128]{1,0:T(8,128)(2,1)S(1)} %bitcast.40, bf16[4096,256]{1,0:T(8,128)(2,1)} %get-tuple-element.17), kind=kOutput, calls=%fused_computation.2 | convolution fusion | flops 1086323712 | bytes 22286336 | tf_op jit(solution)/shard_map/cond/branch_1_fun/kxd,jkd->kxj/dot_general | solution.py:76
  94.0 0.0 copy-done.3
  94.0 0.0 copy-done.1
  94.0 4.3 %fusion.5 = f32[1,1024,128]{2,1,0:T(8,128)S(1)} fusion(pred[1024,4096]{1,0:T(32,128)(4,1)S(1)} %copy-done.1, f32[1024,4096]{1,0:T(8,128)S(1)} %get-tuple-element.40, f32[1024]{0:T(1024)S(1)} %broadcast_maximum_fusion, bf16[4096,256]{1,0:T(8,128)(2,1)S(1)} %copy-done.3), kind=kOutput, calls=%fused_computation.6 | convolution fusion | flops 1094713344 | bytes 22548480 | tf_op jit(solution)/shard_map/cond/branch_1_fun/kxj,jkd->kxd/dot_general | solution.py:83
  98.3 5.6 %fusion.2 = f32[1024]{0:T(1024)S(1)} fusion(pred[1024,4096]{1,0:T(32,128)(4,1)S(1)} %copy-done.1, f32[1024,4096]{1,0:T(8,128)S(1)} %get-tuple-element.40, f32[1024]{0:T(1024)S(1)} %broadcast_maximum_fusion), kind=kLoop, calls=%fused_computation.4 | loop fusion | flops 20970496 | bytes 20979712 | tf_op jit(solution)/shard_map/cond/branch_1_fun/reduce_sum | solution.py:82
  104.0 0.0 copy-start.2
  104.0 0.0 copy-start.4
  104.1 0.2 divide_convert_fusion
  104.3 0.2 copy.25
  104.5 70.5 %all-gather.5.cloned.1.call-done = bf16[1024,4096]{0,1:T(8,128)(2,1)} async-done(((bf16[1024,64]{0,1:T(8,128)(2,1)}), bf16[1024,4096]{0,1:T(8,128)(2,1)}) %all-gather.5.cloned.1.call-update) | async-done | bytes 8388624 | tf_op jit(solution)/shard_map/all_gather | solution.py:123
  175.0 6.3 %convolution_convert_fusion = bf16[128,4096]{1,0:T(8,128)(2,1)S(1)} fusion(bf16[128,1024]{0,1:T(8,128)(2,1)S(1)} %bitcast.41, bf16[1024,4096]{0,1:T(8,128)(2,1)} %all-gather.5.cloned.1.call-done), kind=kOutput, calls=%fused_computation.17 | convolution fusion | flops 1074266112 | bytes 9699328 | tf_op jit(solution)/shard_map/dot_general | solution.py:121
  181.3 0.1 copy.30
  181.3 18.5 %all_to_all.11 = bf16[4,128,1024]{2,1,0:T(8,128)(2,1)S(1)} all-to-all(bf16[4,128,1024]{2,1,0:T(8,128)(2,1)S(1)} %bitcast.39), channel_id=1, replica_groups=mesh['section'=2,'srv'=32,'tp'=4] {'tp'}, dimensions={0} | all-to-all | bytes 2097152 | tf_op jit(solution)/shard_map/all_to_all | solution.py:28
  199.8 0.2 convert_reduce_fusion
  200.0 0.0 copy-done.2
  200.0 0.2 multiply_reduce_fusion
  200.2 6.4 %all_to_all.12 = f32[4,1,128]{2,1,0:T(1,128)S(1)} all-to-all(f32[4,1,128]{2,1,0:T(1,128)S(1)} %broadcast_in_dim.53), channel_id=1, replica_groups=mesh['section'=2,'srv'=32,'tp'=4] {'tp'}, dimensions={0} | all-to-all | bytes 4096 | tf_op jit(solution)/shard_map/all_to_all | solution.py:34
  206.7 0.0 copy-done
  206.7 0.0 copy-done.4
  206.7 1.0 fusion.16
  (7 shorter events, 0.1 us)
Async XLA Ops:
  6.5 200.1 %copy-start = (f32[8,1024]{1,0:T(8,128)S(1)}, f32[8,1024]{1,0:T(8,128)}, u32[]{:S(2)}) copy-start(f32[8,1024]{1,0:T(8,128)} %param.17) | copy-start | bytes 98308
  6.5 81.2 %all-gather.3.cloned.1.call-start = ((), (), s32[]{:S(2)}) async-start(), calls=%async_computation.2 | async-start | bytes 2162688 | tf_op jit(solution)/shard_map/all_gather | solution.py:17
  8.0 167.0 %all-gather.5.cloned.1.call-start = ((), (), s32[]{:S(2)}) async-start(), calls=%async_computation.3 | async-start | bytes 8519680 | tf_op jit(solution)/shard_map/all_gather | solution.py:123
  87.8 6.2 %copy-start.3 = (bf16[4096,256]{1,0:T(8,128)(2,1)S(1)}, bf16[4096,256]{1,0:T(8,128)(2,1)}, u32[]{:S(2)}) copy-start(bf16[4096,256]{1,0:T(8,128)(2,1)} %get-tuple-element.17) | copy-start | bytes 6291460 | tf_op jit(solution)/shard_map/cond
  88.0 6.0 %copy-start.1 = (pred[1024,4096]{1,0:T(32,128)(4,1)S(1)}, pred[1024,4096]{1,0:T(32,128)(4,1)}, u32[]{:S(2)}) copy-start(pred[1024,4096]{1,0:T(32,128)(4,1)} %get-tuple-element.15) | copy-start | bytes 12582916 | tf_op jit(solution)/shard_map/cond
  104.0 96.0 %copy-start.2 = (bf16[128,1024]{1,0:T(8,128)(2,1)S(1)}, bf16[128,1024]{1,0:T(8,128)(2,1)}, u32[]{:S(2)}) copy-start(bf16[128,1024]{1,0:T(8,128)(2,1)} %param.14) | copy-start | bytes 786436
  104.0 102.6 %copy-start.4 = (f32[1024]{0:T(1024)S(1)}, f32[1024]{0:T(1024)}, u32[]{:S(2)}) copy-start(f32[1024]{0:T(1024)} %param.16) | copy-start | bytes 12292
Sparse Core Ops, SparseCore 0:
  10.0 77.7 all-gather.2
  90.5 84.4 all-gather.4
where the time goes:
time: 216 us; the launch traced here: 214 us
  waiting for transfers between devices  137 us (63%)
  blocking collectives  24.9 us (12%)
  other arithmetic  18.6 us (9%)
  matrix products  17.5 us (8%)
  between operations  14.2 us (7%)
    all_gather x1, waiting for transfers between devices, on_device(): lax.all_gather(out_weight, ('section', 'srv'), axis=1, tiled=True)  70.5 us
    all_gather x1, waiting for transfers between devices, in_one_piece(): lax.all_gather(both, axis, axis=dim, tiled=True)  66.1 us
    all_to_all x1, blocking collectives, sent_and_summed(): lax.all_to_all(in_blocks(value, dim, length), axis, 0, 0, tiled=True)  18.5 us
    and x1, other arithmetic, absorb(): (key_pos[None, :] >= row_first[:, None]) & (key_pos[None, :] < row_limit[...  8.79 us
    all_to_all x1, blocking collectives, from_everyone(): return lax.all_to_all(copies, axis, split_axis=0, concat_axis=0, tiled=True)  6.44 us
    dot_general x1, matrix products, on_device(): jnp.dot(attended, lax.all_gather(out_weight, ('section', 'srv'), axis=1,...  6.27 us
    dot_general x1, matrix products, update(): jnp.einsum('kxd,jkd->kxj', grouped, key_heads, preferred_element_type=jnp...  5.97 us
    reduce_sum x1, other arithmetic, update(): total = jnp.sum(weights, axis=-1)  5.58 us
  transfers between devices with their start and end apart: 2, of which 2 were waited for; matrix products, arithmetic and copies ran while one was open for 13% of the time, Pallas kernels for 0%

commit v1 on v0

v1 whole, which is shorter than its diff:
```python
import functools

import jax
import jax.numpy as jnp
from jax import lax
from jax.experimental import pallas as pl
from jax.experimental.pallas import tpu as pltpu
from jax.sharding import PartitionSpec as P

D = 4096
HEAD = 128
BLK = 16
ROWS = 128
NX = 4
NZ = 8
NT = 4
PR = 32
MESH = pl.DeviceIdType.MESH
NEG = -1e30
LOG2E = 1.4426950408889634


def arrive(sem, ref):
    pltpu.make_async_copy(ref, ref, sem).wait()


def nt_dot(a, b):
    return lax.dot_general(a, b, (((1,), (1,)), ((), ())), preferred_element_type=jnp.float32)


def kernel(
    doc_ref, noise_ref, q_ref, k_ref, v_ref, res_ref, wt_ref, gain_ref, shift_ref, out_ref,
    kv, w, bias, m_s, l_s, acc, ab, ob, rb, hid, sq,
    skz, skx1, skx2, sp1, spf, spb, sqf, sqb, sqx, sa, so, ss,
    rkz, rk1, rk2, rp1, rp, rq, rqx, ra, ro, rs,
):
    sec = lax.axis_index("section")
    i = lax.axis_index("srv")
    t = lax.axis_index("tp")
    x = i // NZ
    z = i % NZ
    sgn = 1 - 2 * sec

    def dev(dx=0, dz=0):
        return (sec, ((x + dx + NX) % NX) * NZ + (z + dz + 2 * NZ) % NZ, t)

    def zmod(a):
        return (a + 2 * NZ) % NZ

    def send(src, dst, s, r, to):
        pltpu.make_async_remote_copy(
            src_ref=src, dst_ref=dst, send_sem=s, recv_sem=r, device_id=to, device_id_type=MESH
        ).start()

    kv[x, z, 0] = k_ref[...]
    kv[x, z, 1] = v_ref[...]
    w[x, z] = wt_ref[...]

    peers = [dev(dx=1), dev(dx=-1), dev(dx=2), dev(dz=1), dev(dz=-1), dev(dz=2), dev(dz=-2)]
    peers += [(sec, i, (t + d) % NT) for d in (1, 2, 3)]
    peers += [(1 - sec, i, (t + d) % NT) for d in (0, 1, 2, 3)]
    barrier = pltpu.get_barrier_semaphore()
    for peer in peers:
        pl.semaphore_signal(barrier, inc=1, device_id=peer, device_id_type=MESH)
    pl.semaphore_wait(barrier, len(peers))

    def kv_along_x(zz):
        @pl.when(x < NX - 1)
        def _():
            send(kv.at[x, zz], kv.at[x, zz], skx1.at[zz], rk1.at[zz], dev(dx=1))

        @pl.when((x < NX - 2) & (zz >= z))
        def _():
            send(kv.at[x, zz], kv.at[x, zz], skx2.at[zz], rk2.at[zz], dev(dx=2))

    def late_along_x(zz):
        piece = w.at[x, zz, pl.ds(PR, 64 - PR)]
        for n, dx in enumerate((1, -1, 2)):
            send(piece, piece, sqx.at[n], rqx.at[n], dev(dx=dx))

    for n, dz in enumerate((1, -1, 2, -2)):
        send(kv.at[x, z], kv.at[x, z], skz.at[n], rkz.at[z], dev(dz=dz))
    kv_along_x(z)
    early = w.at[x, z, pl.ds(0, PR)]
    for n, dx in enumerate((1, -1, 2)):
        send(early, early, sp1.at[n], rp1.at[n], dev(dx=dx))
    late = w.at[x, z, pl.ds(PR, 64 - PR)]
    send(late, late, sqf.at[0], rq.at[z], dev(dz=sgn))
    send(late, late, sqb.at[0], rq.at[z], dev(dz=-sgn))
    late_along_x(z)

    def kv_here(dz):
        zz = zmod(z + dz)
        arrive(rkz.at[zz], kv.at[x, zz])
        return zz

    def early_out(zz, xx, sem_f, sem_b, forward, backward):
        piece = w.at[xx, zz, pl.ds(0, PR)]
        if forward:
            send(piece, piece, sem_f, rp.at[zz, xx], dev(dz=sgn))
        if backward:
            send(piece, piece, sem_b, rp.at[zz, xx], dev(dz=-sgn))

    def late_step(k):
        zf = zmod(z - sgn * k)
        piece = w.at[x, zf, pl.ds(PR, 64 - PR)]
        arrive(rq.at[zf], piece)
        if k <= 3:
            send(piece, piece, sqf.at[k], rq.at[zf], dev(dz=sgn))
        late_along_x(zf)
        if k <= 3:
            zb = zmod(z + sgn * k)
            piece = w.at[x, zb, pl.ds(PR, 64 - PR)]
            arrive(rq.at[zb], piece)
            if k <= 2:
                send(piece, piece, sqb.at[k], rq.at[zb], dev(dz=-sgn))
            late_along_x(zb)

    kv_along_x(kv_here(-1))
    kv_along_x(kv_here(1))
    left = kv_here(-2)
    send(kv.at[x, left], kv.at[x, left], skz.at[4], rkz.at[left], dev(dz=1))
    right = kv_here(2)
    send(kv.at[x, right], kv.at[x, right], skz.at[5], rkz.at[right], dev(dz=-1))
    far = zmod(z - 2 * sgn)
    send(kv.at[x, far], kv.at[x, far], skz.at[6], rkz.at[far], dev(dz=2 * sgn))
    kv_along_x(left)
    kv_along_x(right)

    for n, dx in enumerate((1, -1, 2)):
        arrive(rp1.at[n], w.at[(x - dx + NX) % NX, z, pl.ds(0, PR)])

    def first_out(xx, c):
        early_out(z, xx, spf.at[0, xx], spb.at[0, xx], True, True)
        return c

    lax.fori_loop(0, NX, first_out, 0)
    late_step(1)
    kv_along_x(kv_here(-3))
    kv_along_x(kv_here(3))
    kv_along_x(kv_here(4))

    row = i * ROWS + lax.broadcasted_iota(jnp.int32, (ROWS, 1), 0)
    starts, ends, at = [], [], jnp.int32(0)
    for d in range(4):
        starts.append(at)
        at = at + doc_ref[0, d] * BLK
        ends.append(at)
    member = [(row >= starts[d]) & (row < ends[d]) for d in range(4)]
    first = jnp.zeros((ROWS, 1), jnp.int32)
    for d in range(4):
        first = jnp.where(member[d], starts[d], first)
    limit = (row // BLK + 1) * BLK

    def mask_of(xx):
        key = xx * (NZ * ROWS) + lax.broadcasted_iota(jnp.int32, (ROWS, NZ * ROWS), 1)
        bias[...] = jnp.where((key >= first) & (key < limit), 0.0, NEG)

    def unit(xx, h, opening):
        q = q_ref[:, pl.ds(pl.multiple_of(h * HEAD, HEAD), HEAD)]
        keys = kv[xx, :, 0].reshape(NZ * ROWS, HEAD)
        vals = kv[xx, :, 1].reshape(NZ * ROWS, HEAD)
        s = nt_dot(q, keys) * (HEAD ** -0.5 * LOG2E) + bias[...]
        best = jnp.max(s, axis=1, keepdims=True)
        if not opening:
            old = m_s[h][:, :1]
            best = jnp.maximum(best, old)
        p = jnp.exp2(s - best)
        total = jnp.sum(p, axis=1, keepdims=True)
        summed = jnp.dot(p.astype(jnp.bfloat16), vals, preferred_element_type=jnp.float32)
        if not opening:
            alpha = jnp.exp2(old - best)
            total = total + alpha * l_s[h][:, :1]
            summed = summed + alpha * acc[h]
        m_s[h] = jnp.broadcast_to(best, (ROWS, HEAD))
        l_s[h] = jnp.broadcast_to(total, (ROWS, HEAD))
        acc[h] = summed

    def early_step(k, compute):
        def one(xx, c):
            zf = zmod(z - sgn * k)
            arrive(rp.at[zf, xx], w.at[xx, zf, pl.ds(0, PR)])
            if k <= 3:
                early_out(zf, xx, spf.at[min(k, 3), xx], None, True, False)
            if k <= 3:
                zb = zmod(z + sgn * k)
                arrive(rp.at[zb, xx], w.at[xx, zb, pl.ds(0, PR)])
                if k <= 2:
                    early_out(zb, xx, None, spb.at[min(k, 2), xx], False, True)
            if compute is not None:
                compute(2 * xx)
                compute(2 * xx + 1)
            return c

        lax.fori_loop(0, NX, one, 0)

    mask_of(x)
    early_step(1, lambda h: unit(x, h, True))
    late_step(2)

    @pl.when(x >= 1)
    def _():
        def one(zz, c):
            arrive(rk1.at[zz], kv.at[x - 1, zz])
            return c

        lax.fori_loop(0, NZ, one, 0)
        mask_of(x - 1)

    def second(h):
        @pl.when(x >= 1)
        def _():
            unit(x - 1, h, False)

    early_step(2, second)
    late_step(3)

    @pl.when(x >= 2)
    def _():
        def one(zz, c):
            @pl.when(zz >= z)
            def _():
                arrive(rk2.at[zz], kv.at[x - 2, zz])

            @pl.when(zz < z)
            def _():
                kv[x - 2, zz] = jnp.zeros((2, ROWS, HEAD), jnp.bfloat16)

            return c

        lax.fori_loop(0, NZ, one, 0)
        mask_of(x - 2)

    def third(h):
        @pl.when(x >= 2)
        def _():
            unit(x - 2, h, False)

    early_step(3, third)
    late_step(4)

    def attended(h, c):
        ab[sec, :, pl.ds(pl.multiple_of(h * HEAD, HEAD), HEAD)] = (acc[h] / l_s[h]).astype(jnp.bfloat16)
        return c

    lax.fori_loop(0, 8, attended, 0)
    send(ab.at[sec], ab.at[sec], sa.at[0], ra.at[0], (1 - sec, i, t))
    early_step(4, None)
    for n, dx in enumerate((1, -1, 2)):
        arrive(rqx.at[n], w.at[(x - dx + NX) % NX, :, pl.ds(PR, 64 - PR)])
    arrive(ra.at[0], ab.at[1 - sec])

    half = z // 2

    def pair_of(n):
        return (half + n) % 4

    def project(n, c):
        pp = pair_of(n)

        def one(xx, c):
            block = w[xx, pl.ds(2 * pp, 2)].reshape(ROWS, NT * 256)
            o = nt_dot(ab[...].reshape(2 * ROWS, NT * 256), block)
            ob[xx // 2, pp, 0, xx % 2] = o[:ROWS].astype(jnp.bfloat16)
            ob[xx // 2, pp, 1, xx % 2] = o[ROWS:].astype(jnp.bfloat16)
            return c

        lax.fori_loop(0, NX, one, 0)
        for tl in range(2):
            for s2 in range(2):
                to = 2 * sec + tl
                mine = (sec == s2) & (to == t)

                @pl.when(mine)
                def _():
                    pltpu.make_async_copy(ob.at[tl, pp, s2], rb.at[t, pp], ro.at[t, pp]).start()

                @pl.when(jnp.logical_not(mine))
                def _():
                    send(
                        ob.at[tl, pp, s2], rb.at[t, pp], so.at[tl, pp, s2], ro.at[t, pp], (jnp.int32(s2), i, to)
                    )

        return c

    lax.fori_loop(0, 4, project, 0)

    def gathered(n, squares):
        pp = pair_of(n)
        for ts in range(NT):
            arrive(ro.at[ts, pp], rb.at[ts, pp])
        for lo in range(2):
            cols = pl.ds(pl.multiple_of(lo * 512 + pp * 128, 128), 128)
            h = res_ref[:, cols].astype(jnp.float32)
            for ts in range(NT):
                h = h + rb[ts, pp, lo].astype(jnp.float32)
            hid[:, cols] = h
            squares = squares + h * h
        return squares

    squares = lax.fori_loop(0, 4, gathered, jnp.zeros((ROWS, 128), jnp.float32))
    column = jnp.broadcast_to(jnp.sum(squares, axis=1, keepdims=True), (ROWS, 128))
    sq[t] = jnp.transpose(column)[:8]
    for n, d in enumerate((1, 2, 3)):
        send(sq.at[t], sq.at[t], ss.at[n], rs.at[n], (sec, i, (t + d) % NT))
    gains = []
    for d in range(4):
        gains.append(gain_ref[...] * (1.0 + shift_ref[pl.ds(noise_ref[0, d], 1), :]))
    for n, d in enumerate((1, 2, 3)):
        arrive(rs.at[n], sq.at[(t - d + NT) % NT])
    whole = sq[0] + sq[1] + sq[2] + sq[3]
    inverse = jnp.transpose(jnp.broadcast_to(lax.rsqrt(whole[:1] / D + 1e-6), (ROWS, 128)))
    for c in range(8):
        cols = slice(c * 128, c * 128 + 128)
        g = jnp.broadcast_to(gains[0][:, cols], (ROWS, 128))
        for d in range(1, 4):
            g = jnp.where(member[d], gains[d][:, cols], g)
        out_ref[:, cols] = (hid[:, cols] * inverse * g).astype(jnp.bfloat16)

    for n in range(7):
        arrive(skz.at[n], kv.at[0, 0])

    def drain(zz, c):
        @pl.when(x < NX - 1)
        def _():
            arrive(skx1.at[zz], kv.at[0, 0])

        @pl.when((x < NX - 2) & (zz >= z))
        def _():
            arrive(skx2.at[zz], kv.at[0, 0])

        return c

    lax.fori_loop(0, NZ, drain, 0)
    for n in range(3):
        arrive(sp1.at[n], w.at[0, 0, pl.ds(0, PR)])
        arrive(sqx.at[n], w.at[0, :, pl.ds(PR, 64 - PR)])
        arrive(ss.at[n], sq.at[0])

    def drain_early(xx, c):
        for k in range(4):
            arrive(spf.at[k, xx], w.at[0, 0, pl.ds(0, PR)])
        for k in range(3):
            arrive(spb.at[k, xx], w.at[0, 0, pl.ds(0, PR)])
        return c

    lax.fori_loop(0, NX, drain_early, 0)
    for k in range(4):
        arrive(sqf.at[k], w.at[0, 0, pl.ds(PR, 64 - PR)])
    for k in range(3):
        arrive(sqb.at[k], w.at[0, 0, pl.ds(PR, 64 - PR)])
    arrive(sa.at[0], ab.at[0])

    def drain_out(pp, c):
        for tl in range(2):
            for s2 in range(2):
                mine = (sec == s2) & (2 * sec + tl == t)

                @pl.when(jnp.logical_not(mine))
                def _():
                    arrive(so.at[tl, pp, s2], rb.at[0, 0])

        return c

    lax.fori_loop(0, 4, drain_out, 0)


def on_device(queries, keys, values, residual, out_weight, norm_gain, level_shift, doc_lengths, noise_level):
    bf, f32, sem = jnp.bfloat16, jnp.float32, pltpu.SemaphoreType.DMA
    vm = pl.BlockSpec(memory_space=pltpu.VMEM)
    sm = pl.BlockSpec(memory_space=pltpu.SMEM)
    return pl.pallas_call(
        kernel,
        out_shape=jax.ShapeDtypeStruct((ROWS, 1024), bf),
        in_specs=[sm, sm] + [vm] * 7,
        out_specs=vm,
        scratch_shapes=[
            pltpu.VMEM((NX, NZ, 2, ROWS, HEAD), bf),
            pltpu.VMEM((NX, NZ, 64, 1024), bf),
            pltpu.VMEM((ROWS, NZ * ROWS), f32),
            pltpu.VMEM((8, ROWS, HEAD), f32),
            pltpu.VMEM((8, ROWS, HEAD), f32),
            pltpu.VMEM((8, ROWS, HEAD), f32),
            pltpu.VMEM((2, ROWS, 1024), bf),
            pltpu.VMEM((2, 4, 2, 2, ROWS, 128), bf),
            pltpu.VMEM((NT, 4, 2, ROWS, 128), bf),
            pltpu.VMEM((ROWS, 1024), f32),
            pltpu.VMEM((NT, 8, 128), f32),
            sem((7,)), sem((NZ,)), sem((NZ,)), sem((3,)), sem((4, NX)), sem((3, NX)),
            sem((4,)), sem((3,)), sem((3,)), sem((1,)), sem((2, 4, 2)), sem((3,)),
            sem((NZ,)), sem((NZ,)), sem((NZ,)), sem((3,)), sem((NZ, NX)), sem((NZ,)),
            sem((3,)), sem((1,)), sem((NT, 4)), sem((3,)),
        ],
        compiler_params=pltpu.CompilerParams(
            collective_id=0, has_side_effects=True, vmem_limit_bytes=40 << 20
        ),
    )(
        doc_lengths, noise_level, queries, keys, values, residual, out_weight.T,
        norm_gain.reshape(1, 1024), level_shift,
    )


def solution(mesh):
    placed = (
        P(("section", "srv"), "tp"),
        P(("section", "srv"), "tp"),
        P(("section", "srv"), "tp"),
        P(("section", "srv"), "tp"),
        P("tp", ("section", "srv")),
        P("tp"),
        P(None, "tp"),
        P("section", None),
        P("section", None),
    )
    return jax.shard_map(
        on_device,
        mesh=mesh,
        in_specs=placed,
        out_specs=P(("section", "srv"), "tp"),
        check_vma=False,
    )
```

time: 216 us -> 87.7 us (0.41)
  waiting for transfers between devices: 137 us -> 0 us
  Pallas kernels: 0 us -> 80.1 us
  blocking collectives: 24.9 us -> 0 us
  other arithmetic: 18.6 us -> 0 us
  matrix products: 17.5 us -> 0 us
  between operations: 14.2 us -> 0.02 us
  local copies, waits for them, and re-layouts: 1.6 us -> 7.14 us
    all_gather x2 -> x0, waiting for transfers between devices: 137 us -> none  [the longest x1 70.5 us: on_device(): lax.all_gather(out_weight, ('section', 'srv'), axis=1, tiled=True)]
    pallas_call x0 -> x1, Pallas kernels: none -> 80.1 us  [on_device(): pl.pallas_call(kernel, out_shape=jax.ShapeDtypeStruct((ROWS, 1024), bf),...]
    all_to_all x2 -> x0, blocking collectives: 24.9 us -> none  [the longest x1 18.5 us: sent_and_summed(): lax.all_to_all(in_blocks(value, dim, length), axis, 0, 0, tiled=True)]
    dot_general x4 -> x0, matrix products: 17.5 us -> none  [the longest x1 6.27 us: on_device(): jnp.dot(attended, lax.all_gather(out_weight, ('section', 'srv'), axis=1,...]
    and x1 -> x0, other arithmetic: 8.79 us -> none  [absorb(): (key_pos[None, :] >= row_first[:, None]) & (key_pos[None, :] < row_limit[...]
    reduce_sum x5 -> x0, other arithmetic: 6.69 us -> none  [the longest x1 5.58 us: update(): total = jnp.sum(weights, axis=-1)]
    unnamed x7 -> x19, local copies, waits for them, and re-layouts: 1.14 us -> 7.14 us
  transfers between devices with their start and end apart: 2 -> 0, of which waited for: 2 -> 0; matrix products, arithmetic and copies ran while one was open for 13% -> 0% of each run, Pallas kernels for 0% -> 0%
where the time goes in v1:
time: 87.7 us; the launch traced here: 87.3 us
  Pallas kernels  80.1 us (91%)
  local copies, waits for them, and re-layouts  7.14 us (8%)
    pallas_call x1, Pallas kernels, on_device(): pl.pallas_call(kernel, out_shape=jax.ShapeDtypeStruct((ROWS, 1024), bf),...  80.1 us
    unnamed x19, local copies, waits for them, and re-layouts  7.14 us

profile of v1, /device:TPU:1, one launch (start us, length us, event | category | flops | bytes accessed | tf_op | source)
XLA Modules:
  0.0 87.3 jit_solution(14326440349817337777)
XLA Ops:
  0.0 0.0 copy-start.7
  0.0 0.0 copy-start.8
  0.0 0.7 copy-done.7
  0.7 0.0 copy-done.8
  0.7 0.0 copy-start
  0.7 0.9 %copy-done = bf16[128,1024]{1,0:T(8,128)(2,1)S(1)} copy-done((bf16[128,1024]{1,0:T(8,128)(2,1)S(1)}, bf16[128,1024]{1,0:T(8,128)(2,1)}, u32[]{:S(2)}) %copy-start) | copy-done | bytes 262168
  1.6 0.0 copy-start.1
  1.6 0.9 %copy-done.1 = bf16[128,1024]{1,0:T(8,128)(2,1)S(1)} copy-done((bf16[128,1024]{1,0:T(8,128)(2,1)S(1)}, bf16[128,1024]{1,0:T(8,128)(2,1)}, u32[]{:S(2)}) %copy-start.1) | copy-done | bytes 262168
  2.6 0.0 copy-start.2
  2.6 0.9 %copy-done.2 = bf16[1024,64]{0,1:T(8,128)(2,1)S(1)} copy-done((bf16[1024,64]{0,1:T(8,128)(2,1)S(1)}, bf16[1024,64]{0,1:T(8,128)(2,1)}, u32[]{:S(2)}) %copy-start.2) | copy-done | bytes 131096
  3.5 0.0 copy-start.3
  3.5 0.8 copy-done.3
  4.2 0.0 copy-start.4
  4.2 0.8 copy-done.4
  5.0 0.0 copy-start.5
  5.0 0.8 copy-done.5
  5.8 0.0 copy-start.6
  5.8 0.7 copy-done.6
  6.4 80.1 %shard_map.91 = bf16[128,1024]{1,0:T(8,128)(2,1)S(1)} custom-call(s32[1,4]{1,0:T(1,128)S(1)} %copy-done.7, s32[1,4]{1,0:T(1,128)S(1)} %copy-done.8, bf16[128,1024]{1,0:T(8,128)(2,1)S(1)} %copy-done, bf16[128,128]{1,0:T(8,128)(2,1)S(1)} %copy-done.3, bf16[128,128]{1,0:T(8,128)(2,1)S(1)} %copy-done.4, bf16[128,1024]{1,0:T(8,128)(2,1)S(1)} %copy-done.1, ...), custom_call_target="tpu_custom_call" | custom-call | tf_op jit(solution)/shard_map/pallas_call | solution.py:372
  86.6 0.7 copy.11
Async XLA Ops:
  0.0 0.7 copy-start.7
  0.0 0.7 copy-start.8
  0.7 0.9 %copy-start = (bf16[128,1024]{1,0:T(8,128)(2,1)S(1)}, bf16[128,1024]{1,0:T(8,128)(2,1)}, u32[]{:S(2)}) copy-start(bf16[128,1024]{1,0:T(8,128)(2,1)} %q_ref.1) | copy-start | bytes 786436
  1.6 0.9 %copy-start.1 = (bf16[128,1024]{1,0:T(8,128)(2,1)S(1)}, bf16[128,1024]{1,0:T(8,128)(2,1)}, u32[]{:S(2)}) copy-start(bf16[128,1024]{1,0:T(8,128)(2,1)} %res_ref.1) | copy-start | bytes 786436
  2.6 0.9 %copy-start.2 = (bf16[1024,64]{0,1:T(8,128)(2,1)S(1)}, bf16[1024,64]{0,1:T(8,128)(2,1)}, u32[]{:S(2)}) copy-start(bf16[1024,64]{0,1:T(8,128)(2,1)} %param.13) | copy-start | bytes 393220
  3.5 0.8 copy-start.3
  4.2 0.8 copy-start.4
  5.0 0.8 copy-start.5
  5.8 0.7 copy-start.6
